TPU v7x, 512 devices: a whole 4x4x16 slice. The times are simulated.
512 devices in a mesh: hx: 32 (over x, z_lo), hy: 4 (over y), vz: 4 (over z_hi, core).
Axes of the slice: x: 4, y: 4, z: 16 (z_hi: 2, z_lo: 8; z = z_hi * 8 + z_lo), core: 2. Of those that a mesh axis runs over, the one named last changes fastest.
Arguments:
- prognostic: float32 [5, 80, 4, 4, 4, 4096], P(None, 'vz', None, None, 'hy', 'hx'), may hold values from -6 to 6
- metric: float32 [4, 4, 4, 4096], P(None, None, 'hy', 'hx'), may hold values from 0.5 to 2
- first_flux: float32 [5, 5], replicated, may hold values from -2.5 to 2.5
- second_flux: float32 [5, 5], replicated, may hold values from -2.5 to 2.5
- neighbour_face: int32 [4, 4, 4096], P(None, 'hy', 'hx'), may hold values from 0 to 3
- orientation: int32 [4, 4, 4096], P(None, 'hy', 'hx'), may hold values from 0 to 1
- coupling: float32 [4, 80, 4, 4, 4, 4096], P(None, None, 'vz', None, 'hy', 'hx'), may hold values from 0.1 to 1
- damping: float32 [4, 4, 4, 4096], P('vz', None, 'hy', 'hx'), may hold values from 0.005 to 0.05
Outputs:
- updated: float32 [5, 80, 4, 4, 4, 4096], P(None, 'vz', None, None, 'hy', 'hx')
All inputs are finite; a program needn't handle non-finite values.
Results may differ from a plain program's by a relative error of at most 0.0003.
Values sent between devices are 32-bit elements; how exact they have to be, the bound alone decides.
A program may use at most 64 MiB of HBM per device.

v0:
```python
import jax
import jax.numpy as jnp
import numpy as np
from jax import lax
from jax.sharding import PartitionSpec as P

step_size = 0.05
rusanov_speed = 1.0
lift_weight = 6.0
gravity_couple = 0.5
density_couple = 0.3
theta_couple = 0.4


def extended(x, sides, width):
    for axis, dim in sides:
        size, length = (lax.axis_size(axis), x.shape[dim])
        up = [(i, (i + 1) % size) for i in range(size)]
        down = [(j, i) for i, j in up]
        last = lax.slice_in_dim(x, length - width, length, axis=dim)
        initial = lax.slice_in_dim(x, 0, width, axis=dim)
        before = lax.ppermute(last, axis, up)
        after = lax.ppermute(initial, axis, down)
        x = jnp.concatenate([before, x, after], axis=dim)
    return x


def derivative_table():
    points = np.array([-1.0, -1.0 / np.sqrt(5.0), 1.0 / np.sqrt(5.0), 1.0])
    number = points.shape[0]
    barycentric = np.ones(number)
    for source in range(number):
        for another in range(number):
            if another != source:
                barycentric[source] = barycentric[source] / (points[source] - points[another])
    matrix = np.zeros((number, number))
    for target in range(number):
        for source in range(number):
            if target != source:
                matrix[target, source] = (
                    barycentric[source] / barycentric[target] / (points[target] - points[source])
                )
        matrix[target, target] = -np.sum(matrix[target])
    return jnp.asarray(matrix, dtype=jnp.float32)


def face_traces(fields):
    west_face = fields[:, :, :, 0]
    east_face = fields[:, :, :, -1]
    south_face = fields[:, :, 0, :]
    north_face = fields[:, :, -1, :]
    return jnp.stack([west_face, east_face, south_face, north_face], axis=2)


def pick_face(candidates, table_row, flip_row):
    chosen = jnp.zeros(candidates.shape[:2] + candidates.shape[3:], candidates.dtype)
    for option in range(candidates.shape[2]):
        chosen = chosen + jnp.where(table_row == option, candidates[:, :, option], 0.0)
    reverse = chosen[:, :, ::-1]
    return jnp.where(flip_row == 1, reverse, chosen)


def section_values(fields, outer_traces, metric, first_flux, second_flux):
    derivative = derivative_table()
    highest = lax.Precision.HIGHEST
    flux_first = jnp.einsum("fg,gljiab->fljiab", first_flux, fields, precision=highest)
    flux_second = jnp.einsum("fg,gljiab->fljiab", second_flux, fields, precision=highest)
    divergence = jnp.einsum("ci,fljiab->fljcab", derivative, flux_first, precision=highest)
    divergence = divergence + jnp.einsum(
        "cj,fljiab->flciab", derivative, flux_second, precision=highest
    )
    own_traces = face_traces(fields)
    own_first = face_traces(flux_first)
    own_second = face_traces(flux_second)
    own_normal = jnp.stack(
        [-own_first[:, :, 0], own_first[:, :, 1], -own_second[:, :, 2], own_second[:, :, 3]], axis=2
    )
    outer_first = jnp.einsum(
        "fg,glhkab->flhkab", first_flux, outer_traces[:, :, 0:2], precision=highest
    )
    outer_second = jnp.einsum(
        "fg,glhkab->flhkab", second_flux, outer_traces[:, :, 2:4], precision=highest
    )
    outer_normal = jnp.concatenate(
        [
            -outer_first[:, :, 0:1],
            outer_first[:, :, 1:2],
            -outer_second[:, :, 0:1],
            outer_second[:, :, 1:2],
        ],
        axis=2,
    )
    correction = 0.5 * (own_normal - outer_normal) + 0.5 * rusanov_speed * (
        outer_traces - own_traces
    )
    blank_face = jnp.zeros_like(correction[:, :, 0])
    middle_blanks = [blank_face] * (fields.shape[3] - 2)
    across_first = jnp.stack([correction[:, :, 0]] + middle_blanks + [correction[:, :, 1]], axis=3)
    across_second = jnp.stack([correction[:, :, 2]] + middle_blanks + [correction[:, :, 3]], axis=2)
    tendency = metric * (lift_weight * (across_first + across_second) - divergence)
    return fields + step_size * tendency


def level_difference(column_values):
    upper_part = jnp.concatenate([column_values[1:], jnp.zeros_like(column_values[:1])], axis=0)
    lower_part = jnp.concatenate([jnp.zeros_like(column_values[:1]), column_values[:-1]], axis=0)
    return upper_part - lower_part


def solve_unrolled(entry_a, entry_b, centre, entry_d, entry_e, source):
    levels = source.shape[0]
    empty_row = jnp.zeros_like(source[0])
    far_ratio, far_second, far_value = (empty_row, empty_row, empty_row)
    near_ratio, near_second, near_value = (empty_row, empty_row, empty_row)
    ratios, seconds, scaled = ([], [], [])
    for height in range(levels):
        reduced = entry_b[height] - entry_a[height] * far_ratio
        pivot_entry = centre[height] - entry_a[height] * far_second - reduced * near_ratio
        upper_ratio = (entry_d[height] - reduced * near_second) / pivot_entry
        second_ratio = entry_e[height] / pivot_entry
        scaled_value = (
            source[height] - entry_a[height] * far_value - reduced * near_value
        ) / pivot_entry
        far_ratio, far_second, far_value = (near_ratio, near_second, near_value)
        near_ratio, near_second, near_value = (upper_ratio, second_ratio, scaled_value)
        ratios.append(upper_ratio)
        seconds.append(second_ratio)
        scaled.append(scaled_value)
    next_one, next_two = (empty_row, empty_row)
    solution = [None] * levels
    for height in range(levels - 1, -1, -1):
        solved = scaled[height] - ratios[height] * next_one - seconds[height] * next_two
        solution[height] = solved
        next_two, next_one = (next_one, solved)
    return jnp.stack(solution)


def per_device(
    prognostic, metric, first_flux, second_flux, neighbour_face, orientation, coupling, damping
):
    own_traces = face_traces(prognostic)
    extent_first = own_traces.shape[4]
    extent_second = own_traces.shape[5]
    padded = extended(own_traces, (("hx", 5), ("hy", 4)), 1)
    west_outer = pick_face(
        padded[..., 0:extent_first, 1 : extent_second + 1], neighbour_face[0], orientation[0]
    )
    east_outer = pick_face(
        padded[..., 2:, 1 : extent_second + 1], neighbour_face[1], orientation[1]
    )
    south_outer = pick_face(
        padded[..., 1 : extent_first + 1, 0:extent_second], neighbour_face[2], orientation[2]
    )
    north_outer = pick_face(
        padded[..., 1 : extent_first + 1, 2:], neighbour_face[3], orientation[3]
    )
    outer_traces = jnp.stack([west_outer, east_outer, south_outer, north_outer], axis=2)
    section_state = section_values(prognostic, outer_traces, metric, first_flux, second_flux)
    columns = lax.all_to_all(section_state[3:5], "vz", split_axis=2, concat_axis=1, tiled=True)
    source = columns[0] - gravity_couple * level_difference(columns[1])
    centre = coupling[0] + coupling[1] + coupling[2] + coupling[3] + damping[None]
    vertical_speed = solve_unrolled(
        -coupling[0], -coupling[1], centre, -coupling[2], -coupling[3], source
    )
    speed_jump = level_difference(vertical_speed)
    returned = lax.all_to_all(
        jnp.stack([vertical_speed, speed_jump]), "vz", split_axis=1, concat_axis=2, tiled=True
    )
    speed_here = returned[0]
    jump_here = returned[1]
    return jnp.stack(
        [
            section_state[0] - density_couple * jump_here,
            section_state[1],
            section_state[2],
            speed_here,
            section_state[4] - theta_couple * jump_here,
        ]
    )


def solution(mesh):
    placed = (
        P(None, "vz", None, None, "hy", "hx"),
        P(None, None, "hy", "hx"),
        P(),
        P(),
        P(None, "hy", "hx"),
        P(None, "hy", "hx"),
        P(None, None, "vz", None, "hy", "hx"),
        P("vz", None, "hy", "hx"),
    )
    return jax.shard_map(
        per_device,
        mesh=mesh,
        in_specs=placed,
        out_specs=P(None, "vz", None, None, "hy", "hx"),
        check_vma=False,
    )
```

profile of v0, /device:TPU:1, one launch (start us, length us, event | category | flops | bytes accessed | tf_op | source)
XLA Modules:
  0.0 184.2 jit_solution(2517463103171061723)
XLA Ops:
  0.0 1.3 fusion.1374
  1.3 1.3 fusion.1375
  3.1 1.5 fusion.1372
  4.7 2.0 %copy.1166 = f32[5,20,4,4,1,1]{1,3,5,4,2,0:T(4,128)S(1)} copy(f32[5,20,4,4,1,1]{5,0,3,1,4,2:T(8,128)} %get-tuple-element.737) | data formatting | bytes 12800 | tf_op jit(solution)/shard_map/slice | solution.py:20
  6.7 4.4 %collective-permute-start = (f32[5,20,4,4,1,1]{1,3,5,4,2,0:T(4,128)S(1)}, f32[5,20,4,4,1,1]{1,3,5,4,2,0:T(4,128)S(1)}, u32[]{:S(2)}, u32[]{:S(2)}) collective-permute-start(f32[5,20,4,4,1,1]{1,3,5,4,2,0:T(4,128)S(1)} %copy.1166), channel_id=1, source_target_pairs={{0,16},{16,32},{32,48},{48,64},{64,80},{80,96},{96,112},{112,128},... | collective-permute-start | bytes 19208 | tf_op jit(solution)/shard_map/ppermute | solution.py:22
  11.1 1.3 copy.1167
  12.4 13.6 %collective-permute-start.1 = (f32[5,20,4,4,1,1]{1,3,5,4,2,0:T(4,128)}, f32[5,20,4,4,1,1]{1,3,5,4,2,0:T(4,128)}, u32[]{:S(2)}, u32[]{:S(2)}) collective-permute-start(f32[5,20,4,4,1,1]{1,3,5,4,2,0:T(4,128)} %copy.1167), channel_id=1, source_target_pairs={{16,0},{32,16},{48,32},{64,48},{80,64},{96,80},{112,96},{128,112},... | collective-permute-start | bytes 19208 | tf_op jit(solution)/shard_map/ppermute | solution.py:23
  26.0 1.6 fusion.2
  27.7 0.9 fusion.40
  28.6 0.8 slice_bitcast_fusion.2
  30.0 1.6 fusion
  31.8 0.9 slice_negate_fusion.2
  32.7 2.9 %fusion.12 = f32[5,20,4,128,4]{3,4,2,1,0:T(4,128)} fusion(f32[4,4,1,1,1]{1,0,4,3,2:T(4,128)S(1)} %copy-done.59, f32[5,20,4,4,128]{4,0,3,2,1:T(8,128)S(1)} %fusion), kind=kOutput, calls=%fused_computation.22 | convolution fusion | flops 9830400 | bytes 1638464 | tf_op jit(solution)/shard_map/cj,fljiab->flciab/dot_general | solution.py:69
  35.6 0.9 slice_negate_fusion.4
  37.7 2.4 %copy.1168 = f32[5,20,4,4,1,1]{5,0,3,1,4,2:T(8,128)} copy(f32[5,20,4,4,1,1]{1,3,5,4,2,0:T(4,128)S(1)} %collective-permute-done) | data formatting | bytes 12800 | tf_op jit(solution)/shard_map/ppermute | solution.py:22
  40.1 2.2 %copy.1169 = f32[5,20,4,4,1,1]{5,0,3,1,4,2:T(8,128)S(1)} copy(f32[5,20,4,4,1,1]{1,3,5,4,2,0:T(4,128)} %collective-permute-done.1) | data formatting | bytes 12800 | tf_op jit(solution)/shard_map/ppermute | solution.py:23
  42.2 2.4 %pad_maximum_fusion = f32[5,20,4,4,1,130]{5,0,3,1,4,2:T(8,128)S(1)} fusion(f32[5,20,4,4,1,1]{5,0,3,1,4,2:T(8,128)S(1)} %copy.1169, f32[5,20,1,4,1,128]{5,0,3,1,4,2:T(8,128)S(1)} %copy.1567, f32[5,20,1,4,1,128]{5,0,3,1,4,2:T(8,128)S(1)} %copy.1566, f32[5,20,1,4,1,128]{5,0,3,1,4,2:T(8,128)S(1)} %get-tuple-element.861, ...), kind=kLoop, calls=%fused_computation | loop fusion | flops 1040000 | bytes 1664000 | tf_op jit(solution)/shard_map/concatenate | solution.py:24
  45.4 3.2 %collective-permute-start.2 = (f32[5,20,4,4,1,130]{5,3,4,2,1,0:T(4,128)S(1)}, f32[5,20,4,4,1,130]{5,3,4,2,1,0:T(4,128)S(1)}, u32[]{:S(2)}, u32[]{:S(2)}) collective-permute-start(f32[5,20,4,4,1,130]{5,3,4,2,1,0:T(4,128)S(1)} %copy.1170), channel_id=1, source_target_pairs={{0,4},{4,8},{8,12},{12,0},{1,5},{5,9},{9,13},{13,1},{2,6},{6,10},{... | collective-permute-start | bytes 2496008 | tf_op jit(solution)/shard_map/ppermute | solution.py:22
  48.6 3.6 %collective-permute-start.3 = (f32[5,20,4,4,1,130]{5,3,4,2,1,0:T(4,128)S(1)}, f32[5,20,4,4,1,130]{5,3,4,2,1,0:T(4,128)S(1)}, u32[]{:S(2)}, u32[]{:S(2)}) collective-permute-start(f32[5,20,4,4,1,130]{5,3,4,2,1,0:T(4,128)S(1)} %copy.1170), channel_id=1, source_target_pairs={{4,0},{8,4},{12,8},{0,12},{5,1},{9,5},{13,9},{1,13},{6,2},{10,6},{... | collective-permute-start | bytes 2496008 | tf_op jit(solution)/shard_map/ppermute | solution.py:23
  53.0 0.7 fusion.25
  53.8 0.7 convolution_bitcast_fusion.1
  54.6 27.8 %collective-permute-done.2 = f32[5,20,4,4,1,130]{5,3,4,2,1,0:T(4,128)S(1)} collective-permute-done((f32[5,20,4,4,1,130]{5,3,4,2,1,0:T(4,128)S(1)}, f32[5,20,4,4,1,130]{5,3,4,2,1,0:T(4,128)S(1)}, u32[]{:S(2)}, u32[]{:S(2)}) %collective-permute-start.2) | collective-permute-done | bytes 832032 | tf_op jit(solution)/shard_map/ppermute | solution.py:22
  83.3 2.2 %collective-permute-done.3 = f32[5,20,4,4,1,130]{5,3,4,2,1,0:T(4,128)S(1)} collective-permute-done((f32[5,20,4,4,1,130]{5,3,4,2,1,0:T(4,128)S(1)}, f32[5,20,4,4,1,130]{5,3,4,2,1,0:T(4,128)S(1)}, u32[]{:S(2)}, u32[]{:S(2)}) %collective-permute-start.3) | collective-permute-done | bytes 832032 | tf_op jit(solution)/shard_map/ppermute | solution.py:23
  86.4 0.7 convolution_bitcast_fusion.2
  89.1 0.7 copy-done.6
  90.0 2.3 %fusion.10 = f32[5,20,4,4,1,128]{5,3,2,1,0,4:T(4,128)S(1)} fusion(f32[5,20,4,4,1,128]{5,3,2,1,0,4:T(4,128)S(1)} %bitcast.7058, f32[4,4,1,1,1]{1,0,4,3,2:T(4,128)S(1)} %copy-done.59, f32[5,20,4,1,1,128]{5,3,2,1,0,4:T(1,128)S(1)} %copy.1183, f32[5,20,4,1,1,128]{5,3,2,1,0,4:T(1,128)S(1)} %copy.1182, f32[5,20,1,4,1,128]{5,3,2,1,0,4:T(4,128)S(1)} %copy.1185, ...), kind=kOutput, calls=%fused_computation.18 | convolution fusion | flops 12083200 | bytes 4104272 | tf_op jit(solution)/shard_map/ci,fljiab->fljcab/dot_general | solution.py:68
  92.5 0.8 copy.1191
  93.2 15.2 %all-to-all-start = ((f32[2,20,4,4,1,128]{5,3,1,0,4,2:T(4,128)}), f32[2,20,4,4,1,128]{5,3,1,0,4,2:T(4,128)S(1)}, u32[]{:S(2)}, u32[]{:S(2)}) async-start(f32[2,20,4,4,1,128]{5,3,1,0,4,2:T(4,128)} %copy.1191), calls=%async_computation | async-start | bytes 655360 | tf_op jit(solution)/shard_map/all_to_all | solution.py:159
  109.3 0.8 fusion.786
  110.0 0.8 bitcast_subtract_fusion.242
  110.9 0.9 bitcast_subtract_fusion.173
  111.8 11.1 %all-to-all-done = f32[2,20,4,4,1,128]{5,3,1,0,4,2:T(4,128)S(1)} async-done(((f32[2,20,4,4,1,128]{5,3,1,0,4,2:T(4,128)}), f32[2,20,4,4,1,128]{5,3,1,0,4,2:T(4,128)S(1)}, u32[]{:S(2)}, u32[]{:S(2)}) %all-to-all-start) | async-done | bytes 327712 | tf_op jit(solution)/shard_map/all_to_all | solution.py:159
  123.4 0.8 fusion.407
  124.1 0.8 fusion.400
  124.9 0.8 fusion.393
  125.6 0.7 fusion.386
  126.4 0.7 fusion.379
  127.1 0.7 fusion.372
  127.9 0.7 fusion.365
  128.6 0.8 fusion.358
  129.4 0.8 fusion.351
  130.1 0.7 fusion.344
  130.9 0.8 fusion.337
  131.6 0.8 fusion.330
  132.4 0.8 fusion.323
  133.5 0.8 fusion.316
  134.3 0.7 fusion.309
  135.0 0.8 fusion.302
  135.8 0.9 bitcast_subtract_fusion.54
  136.7 1.1 fusion.87
  137.8 1.2 bitcast_multiply_fusion.2
  145.7 1.7 fusion.545
  147.5 0.9 multiply_subtract_fusion.109
  148.4 0.7 multiply_subtract_fusion.107
  149.1 0.7 multiply_subtract_fusion.105
  149.8 0.7 multiply_subtract_fusion.103
  151.2 0.7 multiply_subtract_fusion.99
  151.9 0.7 multiply_subtract_fusion.97
  152.6 0.7 multiply_subtract_fusion.95
  153.3 0.7 multiply_subtract_fusion.93
  154.0 0.7 multiply_subtract_fusion.91
  155.6 1.2 multiply_subtract_fusion.50
  158.1 24.8 %all_to_all.30 = f32[2,80,1,4,1,128]{5,3,4,2,0,1:T(4,128)S(1)} all-to-all(f32[2,80,1,4,1,128]{5,3,4,2,0,1:T(4,128)S(1)} %copy.1550), channel_id=1, replica_groups=mesh['hx'=32,'hy'=4,'vz'=4] {'vz'}, dimensions={1} | all-to-all | bytes 655360 | tf_op jit(solution)/shard_map/all_to_all | solution.py:166
  183.1 1.1 pad_maximum_fusion.2
  (240 shorter events, 18.3 us)
Async XLA Ops:
  0.0 30.0 %copy-start = (f32[5,5]{1,0:T(8,128)S(1)}, f32[5,5]{1,0:T(8,128)}, u32[]{:S(2)}) copy-start(f32[5,5]{1,0:T(8,128)} %param.12) | copy-start | bytes 304
  4.7 21.3 %copy-start.1 = (f32[5,20,4,4,1,128]{5,4,3,2,1,0:T(1,128)S(1)}, f32[5,20,4,4,1,128]{5,4,3,2,1,0:T(1,128)}, u32[]{:S(2)}) copy-start(f32[5,20,4,4,1,128]{5,4,3,2,1,0:T(1,128)} %param.9) | copy-start | bytes 2457604
  4.7 21.3 %copy-start.17 = (f32[5,5]{1,0:T(8,128)S(1)}, f32[5,5]{1,0:T(8,128)}, u32[]{:S(2)}) copy-start(f32[5,5]{1,0:T(8,128)} %param.11) | copy-start | bytes 304
  6.7 31.0 %collective-permute-start = (f32[5,20,4,4,1,1]{1,3,5,4,2,0:T(4,128)S(1)}, f32[5,20,4,4,1,1]{1,3,5,4,2,0:T(4,128)S(1)}, u32[]{:S(2)}, u32[]{:S(2)}) collective-permute-start(f32[5,20,4,4,1,1]{1,3,5,4,2,0:T(4,128)S(1)} %copy.1166), channel_id=1, source_target_pairs={{0,16},{16,32},{32,48},{48,64},{64,80},{80,96},{96,112},{112,128},... | collective-permute-start | bytes 19208 | tf_op jit(solution)/shard_map/ppermute | solution.py:22
  12.4 27.7 %collective-permute-start.1 = (f32[5,20,4,4,1,1]{1,3,5,4,2,0:T(4,128)}, f32[5,20,4,4,1,1]{1,3,5,4,2,0:T(4,128)}, u32[]{:S(2)}, u32[]{:S(2)}) collective-permute-start(f32[5,20,4,4,1,1]{1,3,5,4,2,0:T(4,128)} %copy.1167), channel_id=1, source_target_pairs={{16,0},{32,16},{48,32},{64,48},{80,64},{96,80},{112,96},{128,112},... | collective-permute-start | bytes 19208 | tf_op jit(solution)/shard_map/ppermute | solution.py:23
  44.7 7.5 %copy-start.2 = (f32[5,20,4,4,1,1]{5,0,3,1,4,2:T(8,128)S(1)}, f32[5,20,4,4,1,1]{5,0,3,1,4,2:T(8,128)}, u32[]{:S(2)}) copy-start(f32[5,20,4,4,1,1]{5,0,3,1,4,2:T(8,128)} %copy.1168) | copy-start | bytes 19204
  44.7 7.5 %copy-start.67 = (pred[128]{0:T(512)(128)(4,1)S(1)}, pred[128]{0:T(512)(128)(4,1)}, u32[]{:S(2)}) copy-start(pred[128]{0:T(512)(128)(4,1)} %get-tuple-element.851) | copy-start | bytes 388
  44.7 7.5 %copy-start.68 = (pred[128]{0:T(512)(128)(4,1)S(1)}, pred[128]{0:T(512)(128)(4,1)}, u32[]{:S(2)}) copy-start(pred[128]{0:T(512)(128)(4,1)} %get-tuple-element.852) | copy-start | bytes 388
  44.7 7.5 %copy-start.69 = (pred[128]{0:T(512)(128)(4,1)S(1)}, pred[128]{0:T(512)(128)(4,1)}, u32[]{:S(2)}) copy-start(pred[128]{0:T(512)(128)(4,1)} %get-tuple-element.853) | copy-start | bytes 388
  44.7 7.5 %copy-start.70 = (pred[128]{0:T(512)(128)(4,1)S(1)}, pred[128]{0:T(512)(128)(4,1)}, u32[]{:S(2)}) copy-start(pred[128]{0:T(512)(128)(4,1)} %get-tuple-element.859) | copy-start | bytes 388
  45.4 37.0 %collective-permute-start.2 = (f32[5,20,4,4,1,130]{5,3,4,2,1,0:T(4,128)S(1)}, f32[5,20,4,4,1,130]{5,3,4,2,1,0:T(4,128)S(1)}, u32[]{:S(2)}, u32[]{:S(2)}) collective-permute-start(f32[5,20,4,4,1,130]{5,3,4,2,1,0:T(4,128)S(1)} %copy.1170), channel_id=1, source_target_pairs={{0,4},{4,8},{8,12},{12,0},{1,5},{5,9},{9,13},{13,1},{2,6},{6,10},{... | collective-permute-start | bytes 2496008 | tf_op jit(solution)/shard_map/ppermute | solution.py:22
  48.6 36.9 %collective-permute-start.3 = (f32[5,20,4,4,1,130]{5,3,4,2,1,0:T(4,128)S(1)}, f32[5,20,4,4,1,130]{5,3,4,2,1,0:T(4,128)S(1)}, u32[]{:S(2)}, u32[]{:S(2)}) collective-permute-start(f32[5,20,4,4,1,130]{5,3,4,2,1,0:T(4,128)S(1)} %copy.1170), channel_id=1, source_target_pairs={{4,0},{8,4},{12,8},{0,12},{5,1},{9,5},{13,9},{1,13},{6,2},{10,6},{... | collective-permute-start | bytes 2496008 | tf_op jit(solution)/shard_map/ppermute | solution.py:23
  54.5 28.4 %copy-start.60 = (pred[128]{0:T(512)(128)(4,1)S(1)}, pred[128]{0:T(512)(128)(4,1)}, u32[]{:S(2)}) copy-start(pred[128]{0:T(512)(128)(4,1)} %get-tuple-element.845) | copy-start | bytes 388
  54.5 28.4 %copy-start.61 = (pred[128]{0:T(512)(128)(4,1)S(1)}, pred[128]{0:T(512)(128)(4,1)}, u32[]{:S(2)}) copy-start(pred[128]{0:T(512)(128)(4,1)} %get-tuple-element.846) | copy-start | bytes 388
  54.5 28.4 %copy-start.62 = (pred[128]{0:T(512)(128)(4,1)S(1)}, pred[128]{0:T(512)(128)(4,1)}, u32[]{:S(2)}) copy-start(pred[128]{0:T(512)(128)(4,1)} %get-tuple-element.847) | copy-start | bytes 388
  54.6 28.7 %copy-start.74 = (pred[128]{0:T(512)(128)(4,1)S(1)}, pred[128]{0:T(512)(128)(4,1)}, u32[]{:S(2)}) copy-start(pred[128]{0:T(512)(128)(4,1)} %get-tuple-element.840) | copy-start | bytes 388
  92.3 16.2 %copy-start.8 = (f32[4,80,1,4,1,128]{5,4,3,2,1,0:T(1,128)S(1)}, f32[4,80,1,4,1,128]{5,4,3,2,1,0:T(1,128)}, u32[]{:S(2)}) copy-start(f32[4,80,1,4,1,128]{5,4,3,2,1,0:T(1,128)} %param.15) | copy-start | bytes 1966084
  92.3 16.1 %copy-start.58 = (f32[1,4,1,128]{3,2,1,0:T(1,128)S(1)}, f32[1,4,1,128]{3,2,1,0:T(1,128)}, u32[]{:S(2)}) copy-start(f32[1,4,1,128]{3,2,1,0:T(1,128)} %param.16) | copy-start | bytes 6148
  92.4 16.2 %copy-start.3 = (f32[1,80,1,4,1,128]{5,3,4,2,1,0:T(4,128)S(1)}, f32[1,80,1,4,1,128]{5,3,4,2,1,0:T(4,128)}, u32[]{:S(2)}) copy-start(f32[1,80,1,4,1,128]{5,3,4,2,1,0:T(4,128)} %get-tuple-element.750) | copy-start | bytes 491524
  92.4 16.2 %copy-start.4 = (f32[1,80,1,4,1,128]{5,3,4,2,1,0:T(4,128)S(1)}, f32[1,80,1,4,1,128]{5,3,4,2,1,0:T(4,128)}, u32[]{:S(2)}) copy-start(f32[1,80,1,4,1,128]{5,3,4,2,1,0:T(4,128)} %get-tuple-element.748) | copy-start | bytes 491524
  92.4 16.2 %copy-start.9 = (f32[1,80,1,4,1,128]{5,3,4,2,1,0:T(4,128)S(1)}, f32[1,80,1,4,1,128]{5,3,4,2,1,0:T(4,128)}, u32[]{:S(2)}) copy-start(f32[1,80,1,4,1,128]{5,3,4,2,1,0:T(4,128)} %get-tuple-element.749) | copy-start | bytes 491524
  92.4 16.2 %copy-start.10 = (f32[1,80,1,4,1,128]{5,3,4,2,1,0:T(4,128)S(1)}, f32[1,80,1,4,1,128]{5,3,4,2,1,0:T(4,128)}, u32[]{:S(2)}) copy-start(f32[1,80,1,4,1,128]{5,3,4,2,1,0:T(4,128)} %get-tuple-element.747) | copy-start | bytes 491524
  93.2 29.7 %all-to-all-start = ((f32[2,20,4,4,1,128]{5,3,1,0,4,2:T(4,128)}), f32[2,20,4,4,1,128]{5,3,1,0,4,2:T(4,128)S(1)}, u32[]{:S(2)}, u32[]{:S(2)}) async-start(f32[2,20,4,4,1,128]{5,3,1,0,4,2:T(4,128)} %copy.1191), calls=%async_computation | async-start | bytes 655360 | tf_op jit(solution)/shard_map/all_to_all | solution.py:159
  108.6 14.8 %copy-start.11 = (f32[80,1,4,1,128]{4,2,3,1,0:T(4,128)}, f32[80,1,4,1,128]{4,2,3,1,0:T(4,128)S(1)}, u32[]{:S(2)}) copy-start(f32[80,1,4,1,128]{4,2,3,1,0:T(4,128)S(1)} %bitcast_add_fusion) | copy-start | bytes 491524
  133.1 12.2 %copy-start.18 = (f32[4,128]{1,0:T(4,128)S(1)}, f32[4,128]{1,0:T(4,128)}, u32[]{:S(2)}) copy-start(f32[4,128]{1,0:T(4,128)} %get-tuple-element.692) | copy-start | bytes 6148
  133.1 12.2 %copy-start.19 = (f32[4,128]{1,0:T(4,128)S(1)}, f32[4,128]{1,0:T(4,128)}, u32[]{:S(2)}) copy-start(f32[4,128]{1,0:T(4,128)} %get-tuple-element.693) | copy-start | bytes 6148
  133.2 12.2 %copy-start.20 = (f32[4,128]{1,0:T(4,128)S(1)}, f32[4,128]{1,0:T(4,128)}, u32[]{:S(2)}) copy-start(f32[4,128]{1,0:T(4,128)} %get-tuple-element.698) | copy-start | bytes 6148
  133.2 12.2 %copy-start.21 = (f32[4,128]{1,0:T(4,128)S(1)}, f32[4,128]{1,0:T(4,128)}, u32[]{:S(2)}) copy-start(f32[4,128]{1,0:T(4,128)} %get-tuple-element.699) | copy-start | bytes 6148
  133.2 12.2 %copy-start.22 = (f32[4,128]{1,0:T(4,128)S(1)}, f32[4,128]{1,0:T(4,128)}, u32[]{:S(2)}) copy-start(f32[4,128]{1,0:T(4,128)} %get-tuple-element.704) | copy-start | bytes 6148
  133.2 12.2 %copy-start.23 = (f32[4,128]{1,0:T(4,128)S(1)}, f32[4,128]{1,0:T(4,128)}, u32[]{:S(2)}) copy-start(f32[4,128]{1,0:T(4,128)} %get-tuple-element.705) | copy-start | bytes 6148
  133.2 12.2 %copy-start.24 = (f32[4,128]{1,0:T(4,128)S(1)}, f32[4,128]{1,0:T(4,128)}, u32[]{:S(2)}) copy-start(f32[4,128]{1,0:T(4,128)} %get-tuple-element.573) | copy-start | bytes 6148
  133.2 12.2 %copy-start.25 = (f32[4,128]{1,0:T(4,128)S(1)}, f32[4,128]{1,0:T(4,128)}, u32[]{:S(2)}) copy-start(f32[4,128]{1,0:T(4,128)} %get-tuple-element.574) | copy-start | bytes 6148
  133.2 12.2 %copy-start.26 = (f32[4,128]{1,0:T(4,128)S(1)}, f32[4,128]{1,0:T(4,128)}, u32[]{:S(2)}) copy-start(f32[4,128]{1,0:T(4,128)} %get-tuple-element.579) | copy-start | bytes 6148
  133.2 12.2 %copy-start.27 = (f32[4,128]{1,0:T(4,128)S(1)}, f32[4,128]{1,0:T(4,128)}, u32[]{:S(2)}) copy-start(f32[4,128]{1,0:T(4,128)} %get-tuple-element.580) | copy-start | bytes 6148
  133.2 12.2 %copy-start.28 = (f32[4,128]{1,0:T(4,128)S(1)}, f32[4,128]{1,0:T(4,128)}, u32[]{:S(2)}) copy-start(f32[4,128]{1,0:T(4,128)} %get-tuple-element.585) | copy-start | bytes 6148
  133.2 12.2 %copy-start.29 = (f32[4,128]{1,0:T(4,128)S(1)}, f32[4,128]{1,0:T(4,128)}, u32[]{:S(2)}) copy-start(f32[4,128]{1,0:T(4,128)} %get-tuple-element.586) | copy-start | bytes 6148
  133.3 12.2 %copy-start.30 = (f32[4,128]{1,0:T(4,128)S(1)}, f32[4,128]{1,0:T(4,128)}, u32[]{:S(2)}) copy-start(f32[4,128]{1,0:T(4,128)} %get-tuple-element.591) | copy-start | bytes 6148
  133.3 12.2 %copy-start.31 = (f32[4,128]{1,0:T(4,128)S(1)}, f32[4,128]{1,0:T(4,128)}, u32[]{:S(2)}) copy-start(f32[4,128]{1,0:T(4,128)} %get-tuple-element.592) | copy-start | bytes 6148
  133.3 12.2 %copy-start.32 = (f32[4,128]{1,0:T(4,128)S(1)}, f32[4,128]{1,0:T(4,128)}, u32[]{:S(2)}) copy-start(f32[4,128]{1,0:T(4,128)} %get-tuple-element.597) | copy-start | bytes 6148
  133.3 12.2 %copy-start.33 = (f32[4,128]{1,0:T(4,128)S(1)}, f32[4,128]{1,0:T(4,128)}, u32[]{:S(2)}) copy-start(f32[4,128]{1,0:T(4,128)} %get-tuple-element.598) | copy-start | bytes 6148
  133.3 12.2 %copy-start.34 = (f32[4,128]{1,0:T(4,128)S(1)}, f32[4,128]{1,0:T(4,128)}, u32[]{:S(2)}) copy-start(f32[4,128]{1,0:T(4,128)} %get-tuple-element.603) | copy-start | bytes 6148
  133.3 12.2 %copy-start.35 = (f32[4,128]{1,0:T(4,128)S(1)}, f32[4,128]{1,0:T(4,128)}, u32[]{:S(2)}) copy-start(f32[4,128]{1,0:T(4,128)} %get-tuple-element.604) | copy-start | bytes 6148
  133.3 12.2 %copy-start.36 = (f32[4,128]{1,0:T(4,128)S(1)}, f32[4,128]{1,0:T(4,128)}, u32[]{:S(2)}) copy-start(f32[4,128]{1,0:T(4,128)} %get-tuple-element.609) | copy-start | bytes 6148
  133.3 12.2 %copy-start.37 = (f32[4,128]{1,0:T(4,128)S(1)}, f32[4,128]{1,0:T(4,128)}, u32[]{:S(2)}) copy-start(f32[4,128]{1,0:T(4,128)} %get-tuple-element.610) | copy-start | bytes 6148
  133.3 12.2 %copy-start.38 = (f32[4,128]{1,0:T(4,128)S(1)}, f32[4,128]{1,0:T(4,128)}, u32[]{:S(2)}) copy-start(f32[4,128]{1,0:T(4,128)} %get-tuple-element.615) | copy-start | bytes 6148
  133.3 12.2 %copy-start.39 = (f32[4,128]{1,0:T(4,128)S(1)}, f32[4,128]{1,0:T(4,128)}, u32[]{:S(2)}) copy-start(f32[4,128]{1,0:T(4,128)} %get-tuple-element.616) | copy-start | bytes 6148
  133.4 12.2 %copy-start.40 = (f32[4,128]{1,0:T(4,128)S(1)}, f32[4,128]{1,0:T(4,128)}, u32[]{:S(2)}) copy-start(f32[4,128]{1,0:T(4,128)} %get-tuple-element.621) | copy-start | bytes 6148
  133.4 12.2 %copy-start.41 = (f32[4,128]{1,0:T(4,128)S(1)}, f32[4,128]{1,0:T(4,128)}, u32[]{:S(2)}) copy-start(f32[4,128]{1,0:T(4,128)} %get-tuple-element.622) | copy-start | bytes 6148
  133.4 12.2 %copy-start.42 = (f32[4,128]{1,0:T(4,128)S(1)}, f32[4,128]{1,0:T(4,128)}, u32[]{:S(2)}) copy-start(f32[4,128]{1,0:T(4,128)} %get-tuple-element.627) | copy-start | bytes 6148
  133.4 12.2 %copy-start.43 = (f32[4,128]{1,0:T(4,128)S(1)}, f32[4,128]{1,0:T(4,128)}, u32[]{:S(2)}) copy-start(f32[4,128]{1,0:T(4,128)} %get-tuple-element.628) | copy-start | bytes 6148
  133.4 12.2 %copy-start.44 = (f32[4,128]{1,0:T(4,128)S(1)}, f32[4,128]{1,0:T(4,128)}, u32[]{:S(2)}) copy-start(f32[4,128]{1,0:T(4,128)} %get-tuple-element.633) | copy-start | bytes 6148
  133.4 12.2 %copy-start.45 = (f32[4,128]{1,0:T(4,128)S(1)}, f32[4,128]{1,0:T(4,128)}, u32[]{:S(2)}) copy-start(f32[4,128]{1,0:T(4,128)} %get-tuple-element.634) | copy-start | bytes 6148
  133.4 12.2 %copy-start.46 = (f32[4,128]{1,0:T(4,128)S(1)}, f32[4,128]{1,0:T(4,128)}, u32[]{:S(2)}) copy-start(f32[4,128]{1,0:T(4,128)} %get-tuple-element.860) | copy-start | bytes 6148
  133.4 12.2 %copy-start.47 = (f32[4,128]{1,0:T(4,128)S(1)}, f32[4,128]{1,0:T(4,128)}, u32[]{:S(2)}) copy-start(f32[4,128]{1,0:T(4,128)} %get-tuple-element.499) | copy-start | bytes 6148
  133.4 12.2 %copy-start.48 = (f32[4,128]{1,0:T(4,128)S(1)}, f32[4,128]{1,0:T(4,128)}, u32[]{:S(2)}) copy-start(f32[4,128]{1,0:T(4,128)} %get-tuple-element.502) | copy-start | bytes 6148
  133.4 12.2 %copy-start.49 = (f32[4,128]{1,0:T(4,128)S(1)}, f32[4,128]{1,0:T(4,128)}, u32[]{:S(2)}) copy-start(f32[4,128]{1,0:T(4,128)} %get-tuple-element.507) | copy-start | bytes 6148
  133.5 12.2 %copy-start.50 = (f32[4,128]{1,0:T(4,128)S(1)}, f32[4,128]{1,0:T(4,128)}, u32[]{:S(2)}) copy-start(f32[4,128]{1,0:T(4,128)} %get-tuple-element.508) | copy-start | bytes 6148
  133.5 12.2 %copy-start.51 = (f32[4,128]{1,0:T(4,128)S(1)}, f32[4,128]{1,0:T(4,128)}, u32[]{:S(2)}) copy-start(f32[4,128]{1,0:T(4,128)} %get-tuple-element.513) | copy-start | bytes 6148
  133.5 12.2 %copy-start.52 = (f32[4,128]{1,0:T(4,128)S(1)}, f32[4,128]{1,0:T(4,128)}, u32[]{:S(2)}) copy-start(f32[4,128]{1,0:T(4,128)} %get-tuple-element.514) | copy-start | bytes 6148
  133.5 12.2 %copy-start.53 = (f32[4,128]{1,0:T(4,128)S(1)}, f32[4,128]{1,0:T(4,128)}, u32[]{:S(2)}) copy-start(f32[4,128]{1,0:T(4,128)} %get-tuple-element.519) | copy-start | bytes 6148
  133.5 12.2 %copy-start.54 = (f32[4,128]{1,0:T(4,128)S(1)}, f32[4,128]{1,0:T(4,128)}, u32[]{:S(2)}) copy-start(f32[4,128]{1,0:T(4,128)} %get-tuple-element.520) | copy-start | bytes 6148
  133.5 12.2 %copy-start.55 = (f32[4,128]{1,0:T(4,128)S(1)}, f32[4,128]{1,0:T(4,128)}, u32[]{:S(2)}) copy-start(f32[4,128]{1,0:T(4,128)} %get-tuple-element.525) | copy-start | bytes 6148
  133.5 12.2 %copy-start.56 = (f32[4,128]{1,0:T(4,128)S(1)}, f32[4,128]{1,0:T(4,128)}, u32[]{:S(2)}) copy-start(f32[4,128]{1,0:T(4,128)} %get-tuple-element.526) | copy-start | bytes 6148
  133.5 12.2 %copy-start.57 = (f32[4,128]{1,0:T(4,128)S(1)}, f32[4,128]{1,0:T(4,128)}, u32[]{:S(2)}) copy-start(f32[4,128]{1,0:T(4,128)} %get-tuple-element.531) | copy-start | bytes 6148
  (20 other events, 29.5 us)
where the time goes:
time: 186 us; the launch traced here: 184 us
  other arithmetic  46.4 us (25%)
  waiting for transfers between devices  41.2 us (22%)
  starting transfers between devices  40 us (22%)
  blocking collectives  24.8 us (13%)
  local copies, waits for them, and re-layouts  20.3 us (11%)
  matrix products  9.88 us (5%)
    ppermute x2, waiting for transfers between devices, extended(): before = lax.ppermute(last, axis, up)  27.8 us
    all_to_all x1, blocking collectives, per_device(): lax.all_to_all(jnp.stack([vertical_speed, speed_jump]), 'vz', split_axis=...  24.8 us
    ppermute x2, starting transfers between devices, extended(): after = lax.ppermute(initial, axis, down)  17.2 us
    all_to_all x1, starting transfers between devices, per_device(): lax.all_to_all(section_state[3:5], 'vz', split_axis=2, concat_axis=1, til...  15.2 us
    sub x34, other arithmetic, solve_unrolled(): scaled[height] - ratios[height] * next_one - seconds[height] * next_two  14.2 us
    div x21, other arithmetic, solve_unrolled(): (source[height] - entry_a[height] * far_value - reduced * near_value) / p...  13.8 us
    all_to_all x1, waiting for transfers between devices, per_device(): lax.all_to_all(section_state[3:5], 'vz', split_axis=2, concat_axis=1, til...  11.1 us
    ppermute x2, starting transfers between devices, extended(): before = lax.ppermute(last, axis, up)  7.56 us
  transfers between devices with their start and end apart: 5, of which 3 were waited for; matrix products, arithmetic and copies ran while one was open for 12% of the time, Pallas kernels for 0%

commit v1 on v0

--- a/solution.py
+++ b/solution.py
@@ -3,6 +3,7 @@
 import numpy as np
 from jax import lax
 from jax.sharding import PartitionSpec as P
+from jax.lax import all_to_all, axis_size
 
 step_size = 0.05
 rusanov_speed = 1.0
@@ -10,6 +11,9 @@
 gravity_couple = 0.5
 density_couple = 0.3
 theta_couple = 0.4
+perform_cube = lambda v0: jnp.concatenate(
+    all_to_all(jnp.stack(jnp.split(v0, axis_size("vz"), 2), axis=0), "vz", 0, 0), 1
+)
 
 
 def extended(x, sides, width):
@@ -156,7 +160,7 @@
     )
     outer_traces = jnp.stack([west_outer, east_outer, south_outer, north_outer], axis=2)
     section_state = section_values(prognostic, outer_traces, metric, first_flux, second_flux)
-    columns = lax.all_to_all(section_state[3:5], "vz", split_axis=2, concat_axis=1, tiled=True)
+    columns = perform_cube(section_state[3:5])
     source = columns[0] - gravity_couple * level_difference(columns[1])
     centre = coupling[0] + coupling[1] + coupling[2] + coupling[3] + damping[None]
     vertical_speed = solve_unrolled(

time: 186 us -> 179 us (0.962)
  blocking collectives: 24.8 us -> 0 us
  waiting for transfers between devices: 41.2 us -> 58.8 us
  starting transfers between devices: 40 us -> 50.4 us
  other arithmetic: 46.4 us -> 39.8 us
  local copies, waits for them, and re-layouts: 20.3 us -> 18 us
    all_to_all x1 -> x0, blocking collectives: 24.8 us -> none  [per_device(): lax.all_to_all(jnp.stack([vertical_speed, speed_jump]), 'vz', split_axis=...]
    all_to_all x1 -> x2, waiting for transfers between devices: 11.1 us -> 28.6 us  [the longest x1 14.4 us: per_device(): lax.all_to_all(jnp.stack([vertical_speed, speed_jump]), 'vz', split_axis=...]
    all_to_all x1 -> x2, starting transfers between devices: 15.2 us -> 25.6 us  [the longest x1 15.3 us: all_to_all(jnp.stack(jnp.split(v0, axis_size('vz'), 2), axis=0), 'vz', 0, 0)]
    sub x34 -> x19, other arithmetic: 14.2 us -> 7.92 us  [solve_unrolled(): scaled[height] - ratios[height] * next_one - seconds[height] * next_two]
    mul x4 -> x0, other arithmetic: 2.54 us -> none  [the longest x1 1.17 us: solve_unrolled(): entry_a[height] * far_value]
    div x21 -> x22, other arithmetic: 13.8 us -> 15.2 us  [solve_unrolled(): (source[height] - entry_a[height] * far_value - reduced * near_value) / p...]
  transfers between devices with their start and end apart: 5 -> 6, of which waited for: 3 -> 4; matrix products, arithmetic and copies ran while one was open for 12% -> 10% of each run, Pallas kernels for 0% -> 0%
where the time goes in v1:
time: 179 us; the launch traced here: 178 us
  waiting for transfers between devices  58.8 us (33%)
  starting transfers between devices  50.4 us (28%)
  other arithmetic  39.8 us (22%)
  local copies, waits for them, and re-layouts  18 us (10%)
  matrix products  9.87 us (6%)
    ppermute x2, waiting for transfers between devices, extended(): before = lax.ppermute(last, axis, up)  27.9 us
    ppermute x2, starting transfers between devices, extended(): after = lax.ppermute(initial, axis, down)  17.2 us
    all_to_all x1, starting transfers between devices, all_to_all(jnp.stack(jnp.split(v0, axis_size('vz'), 2), axis=0), 'vz', 0, 0)  15.3 us
    div x22, other arithmetic, solve_unrolled(): (source[height] - entry_a[height] * far_value - reduced * near_value) / p...  15.2 us
    all_to_all x1, waiting for transfers between devices, per_device(): lax.all_to_all(jnp.stack([vertical_speed, speed_jump]), 'vz', split_axis=...  14.4 us
    all_to_all x1, waiting for transfers between devices, all_to_all(jnp.stack(jnp.split(v0, axis_size('vz'), 2), axis=0), 'vz', 0, 0)  14.1 us
    all_to_all x1, starting transfers between devices, per_device(): lax.all_to_all(jnp.stack([vertical_speed, speed_jump]), 'vz', split_axis=...  10.4 us
    sub x19, other arithmetic, solve_unrolled(): scaled[height] - ratios[height] * next_one - seconds[height] * next_two  7.92 us
  transfers between devices with their start and end apart: 6, of which 4 were waited for; matrix products, arithmetic and copies ran while one was open for 10% of the time, Pallas kernels for 0%

profile of v1, /device:TPU:1, one launch (start us, length us, event | category | flops | bytes accessed | tf_op | source)
XLA Modules:
  0.0 177.9 jit_solution(3143081680801476)
XLA Ops:
  0.0 1.3 fusion.1356
  1.3 1.3 fusion.1357
  3.1 1.5 fusion.1355
  4.7 2.0 %copy.789 = f32[5,20,4,4,1,1]{1,3,5,4,2,0:T(4,128)S(1)} copy(f32[5,20,4,4,1,1]{5,0,3,1,4,2:T(8,128)} %get-tuple-element.704) | data formatting | bytes 12800 | tf_op jit(solution)/shard_map/slice | solution.py:24
  6.7 4.4 %collective-permute-start = (f32[5,20,4,4,1,1]{1,3,5,4,2,0:T(4,128)S(1)}, f32[5,20,4,4,1,1]{1,3,5,4,2,0:T(4,128)S(1)}, u32[]{:S(2)}, u32[]{:S(2)}) collective-permute-start(f32[5,20,4,4,1,1]{1,3,5,4,2,0:T(4,128)S(1)} %copy.789), channel_id=1, source_target_pairs={{0,16},{16,32},{32,48},{48,64},{64,80},{80,96},{96,112},{112,128},... | collective-permute-start | bytes 19208 | tf_op jit(solution)/shard_map/ppermute | solution.py:26
  11.0 1.3 copy.790
  12.4 13.6 %collective-permute-start.1 = (f32[5,20,4,4,1,1]{1,3,5,4,2,0:T(4,128)}, f32[5,20,4,4,1,1]{1,3,5,4,2,0:T(4,128)S(1)}, u32[]{:S(2)}, u32[]{:S(2)}) collective-permute-start(f32[5,20,4,4,1,1]{1,3,5,4,2,0:T(4,128)} %copy.790), channel_id=1, source_target_pairs={{16,0},{32,16},{48,32},{64,48},{80,64},{96,80},{112,96},{128,112},... | collective-permute-start | bytes 19208 | tf_op jit(solution)/shard_map/ppermute | solution.py:27
  26.0 1.6 fusion.2
  27.7 0.9 fusion.40
  28.6 0.8 slice_bitcast_fusion.2
  29.9 1.6 fusion
  31.7 0.9 slice_negate_fusion.2
  32.6 2.9 %fusion.12 = f32[5,20,4,128,4]{3,4,2,1,0:T(4,128)} fusion(f32[4,4,1,1,1]{1,0,4,3,2:T(4,128)S(1)} %copy-done.22, f32[5,20,4,4,128]{4,0,3,2,1:T(8,128)S(1)} %fusion), kind=kOutput, calls=%fused_computation.22 | convolution fusion | flops 9830400 | bytes 1638464 | tf_op jit(solution)/shard_map/cj,fljiab->flciab/dot_general | solution.py:73
  36.6 2.4 %copy.791 = f32[5,20,4,4,1,1]{5,0,3,1,4,2:T(8,128)} copy(f32[5,20,4,4,1,1]{1,3,5,4,2,0:T(4,128)S(1)} %collective-permute-done) | data formatting | bytes 12800 | tf_op jit(solution)/shard_map/ppermute | solution.py:26
  39.0 1.4 copy.792
  40.4 2.4 %pad_maximum_fusion = f32[5,20,4,4,1,130]{5,0,3,1,4,2:T(8,128)S(1)} fusion(f32[5,20,4,4,1,1]{5,0,3,1,4,2:T(8,128)S(1)} %copy.792, f32[5,20,1,4,1,128]{5,0,3,1,4,2:T(8,128)S(1)} %copy.1072, f32[5,20,1,4,1,128]{5,0,3,1,4,2:T(8,128)S(1)} %copy.1071, f32[5,20,1,4,1,128]{5,0,3,1,4,2:T(8,128)S(1)} %get-tuple-element.984, ...), kind=kLoop, calls=%fused_computation | loop fusion | flops 1040000 | bytes 1664000 | tf_op jit(solution)/shard_map/concatenate | solution.py:28
  43.5 3.2 %collective-permute-start.2 = (f32[5,20,4,4,1,130]{5,3,4,2,1,0:T(4,128)S(1)}, f32[5,20,4,4,1,130]{5,3,4,2,1,0:T(4,128)S(1)}, u32[]{:S(2)}, u32[]{:S(2)}) collective-permute-start(f32[5,20,4,4,1,130]{5,3,4,2,1,0:T(4,128)S(1)} %copy.793), channel_id=1, source_target_pairs={{0,4},{4,8},{8,12},{12,0},{1,5},{5,9},{9,13},{13,1},{2,6},{6,10},{... | collective-permute-start | bytes 2496008 | tf_op jit(solution)/shard_map/ppermute | solution.py:26
  46.7 3.6 %collective-permute-start.3 = (f32[5,20,4,4,1,130]{5,3,4,2,1,0:T(4,128)S(1)}, f32[5,20,4,4,1,130]{5,3,4,2,1,0:T(4,128)S(1)}, u32[]{:S(2)}, u32[]{:S(2)}) collective-permute-start(f32[5,20,4,4,1,130]{5,3,4,2,1,0:T(4,128)S(1)} %copy.793), channel_id=1, source_target_pairs={{4,0},{8,4},{12,8},{0,12},{5,1},{9,5},{13,9},{1,13},{6,2},{10,6},{... | collective-permute-start | bytes 2496008 | tf_op jit(solution)/shard_map/ppermute | solution.py:27
  51.0 0.7 fusion.25
  51.8 0.7 convolution_bitcast_fusion.1
  52.6 27.9 %collective-permute-done.2 = f32[5,20,4,4,1,130]{5,3,4,2,1,0:T(4,128)S(1)} collective-permute-done((f32[5,20,4,4,1,130]{5,3,4,2,1,0:T(4,128)S(1)}, f32[5,20,4,4,1,130]{5,3,4,2,1,0:T(4,128)S(1)}, u32[]{:S(2)}, u32[]{:S(2)}) %collective-permute-start.2) | collective-permute-done | bytes 832032 | tf_op jit(solution)/shard_map/ppermute | solution.py:26
  81.4 2.3 %collective-permute-done.3 = f32[5,20,4,4,1,130]{5,3,4,2,1,0:T(4,128)S(1)} collective-permute-done((f32[5,20,4,4,1,130]{5,3,4,2,1,0:T(4,128)S(1)}, f32[5,20,4,4,1,130]{5,3,4,2,1,0:T(4,128)S(1)}, u32[]{:S(2)}, u32[]{:S(2)}) %collective-permute-start.3) | collective-permute-done | bytes 832032 | tf_op jit(solution)/shard_map/ppermute | solution.py:27
  84.6 0.7 convolution_bitcast_fusion.2
  87.2 0.7 copy-done.8
  88.1 2.3 %fusion.10 = f32[5,20,4,4,1,128]{5,3,2,1,0,4:T(4,128)S(1)} fusion(f32[5,20,4,4,1,128]{5,3,2,1,0,4:T(4,128)S(1)} %bitcast.7428, f32[4,4,1,1,1]{1,0,4,3,2:T(4,128)S(1)} %copy-done.22, f32[5,20,4,1,1,128]{5,3,2,1,0,4:T(1,128)S(1)} %copy.806, f32[5,20,4,1,1,128]{5,3,2,1,0,4:T(1,128)S(1)} %copy.805, f32[5,20,1,4,1,128]{5,3,2,1,0,4:T(4,128)S(1)} %copy.808, ...), kind=kOutput, calls=%fused_computation.18 | convolution fusion | flops 12083200 | bytes 4104272 | tf_op jit(solution)/shard_map/ci,fljiab->fljcab/dot_general | solution.py:72
  90.5 0.8 pad_maximum_fusion.11
  91.3 15.3 %all-to-all-start = ((f32[4,2,20,1,4,1,128]{6,4,2,1,5,3,0:T(4,128)}), f32[4,2,20,1,4,1,128]{6,4,2,1,5,3,0:T(4,128)S(1)}, u32[]{:S(2)}, u32[]{:S(2)}) async-start(f32[4,2,20,1,4,1,128]{6,4,2,1,5,3,0:T(4,128)} %pad_maximum_fusion.11), calls=%async_computation | async-start | bytes 655360 | tf_op jit(solution)/shard_map/all_to_all | solution.py:15
  106.9 14.1 %all-to-all-done = f32[4,2,20,1,4,1,128]{6,4,2,1,5,3,0:T(4,128)S(1)} async-done(((f32[4,2,20,1,4,1,128]{6,4,2,1,5,3,0:T(4,128)}), f32[4,2,20,1,4,1,128]{6,4,2,1,5,3,0:T(4,128)S(1)}, u32[]{:S(2)}, u32[]{:S(2)}) %all-to-all-start) | async-done | bytes 327712 | tf_op jit(solution)/shard_map/all_to_all | solution.py:15
  122.6 0.8 multiply_subtract_fusion.95
  123.4 0.7 multiply_subtract_fusion.93
  124.1 0.7 multiply_subtract_fusion.91
  124.8 0.7 multiply_subtract_fusion.89
  125.5 0.7 multiply_subtract_fusion.87
  126.2 0.7 multiply_subtract_fusion.85
  126.9 0.7 multiply_subtract_fusion.83
  127.6 0.7 multiply_subtract_fusion.81
  128.3 1.2 constant_dynamic-update-slice_fusion.79
  130.3 0.8 fusion.424
  131.1 0.8 fusion.417
  131.9 0.8 fusion.410
  132.7 0.8 fusion.403
  133.4 0.8 fusion.396
  134.2 0.8 fusion.389
  135.0 0.8 fusion.382
  135.8 0.8 fusion.375
  136.6 0.8 fusion.368
  137.3 0.8 fusion.361
  138.1 0.8 fusion.354
  138.9 0.8 fusion.347
  139.7 0.8 fusion.340
  140.5 0.8 fusion.333
  141.3 0.8 fusion.326
  142.0 0.8 fusion.319
  142.8 0.8 fusion.312
  143.6 0.8 fusion.305
  144.4 1.0 bitcast_subtract_fusion.61
  145.4 1.3 bitcast_subtract_fusion.15
  146.7 0.7 bitcast_subtract_fusion.13
  147.4 1.2 multiply_subtract_fusion.37
  148.6 0.8 multiply_subtract_fusion.35
  151.0 0.8 pad_maximum_fusion.12
  151.8 10.4 %all-to-all-start.1 = ((f32[2,80,1,4,1,128]{5,3,4,2,0,1:T(4,128)}), f32[2,80,1,4,1,128]{5,3,4,2,0,1:T(4,128)S(1)}, u32[]{:S(2)}, u32[]{:S(2)}) async-start(f32[2,80,1,4,1,128]{5,3,4,2,0,1:T(4,128)} %pad_maximum_fusion.12), calls=%async_computation.1 | async-start | bytes 655360 | tf_op jit(solution)/shard_map/all_to_all | solution.py:170
  162.2 14.4 %all-to-all-done.1 = f32[2,80,1,4,1,128]{5,3,4,2,0,1:T(4,128)S(1)} async-done(((f32[2,80,1,4,1,128]{5,3,4,2,0,1:T(4,128)}), f32[2,80,1,4,1,128]{5,3,4,2,0,1:T(4,128)S(1)}, u32[]{:S(2)}, u32[]{:S(2)}) %all-to-all-start.1) | async-done | bytes 327712 | tf_op jit(solution)/shard_map/all_to_all | solution.py:170
  176.8 1.1 pad_maximum_fusion.2
  (202 shorter events, 11.4 us)
Async XLA Ops:
  0.0 29.9 %copy-start = (f32[5,5]{1,0:T(8,128)S(1)}, f32[5,5]{1,0:T(8,128)}, u32[]{:S(2)}) copy-start(f32[5,5]{1,0:T(8,128)} %param.12) | copy-start | bytes 304
  4.7 21.3 %copy-start.1 = (f32[5,20,4,4,1,128]{5,4,3,2,1,0:T(1,128)S(1)}, f32[5,20,4,4,1,128]{5,4,3,2,1,0:T(1,128)}, u32[]{:S(2)}) copy-start(f32[5,20,4,4,1,128]{5,4,3,2,1,0:T(1,128)} %param.9) | copy-start | bytes 2457604
  4.7 21.3 %copy-start.20 = (f32[5,5]{1,0:T(8,128)S(1)}, f32[5,5]{1,0:T(8,128)}, u32[]{:S(2)}) copy-start(f32[5,5]{1,0:T(8,128)} %param.11) | copy-start | bytes 304
  6.7 30.0 %collective-permute-start = (f32[5,20,4,4,1,1]{1,3,5,4,2,0:T(4,128)S(1)}, f32[5,20,4,4,1,1]{1,3,5,4,2,0:T(4,128)S(1)}, u32[]{:S(2)}, u32[]{:S(2)}) collective-permute-start(f32[5,20,4,4,1,1]{1,3,5,4,2,0:T(4,128)S(1)} %copy.789), channel_id=1, source_target_pairs={{0,16},{16,32},{32,48},{48,64},{64,80},{80,96},{96,112},{112,128},... | collective-permute-start | bytes 19208 | tf_op jit(solution)/shard_map/ppermute | solution.py:26
  12.4 26.6 %collective-permute-start.1 = (f32[5,20,4,4,1,1]{1,3,5,4,2,0:T(4,128)}, f32[5,20,4,4,1,1]{1,3,5,4,2,0:T(4,128)S(1)}, u32[]{:S(2)}, u32[]{:S(2)}) collective-permute-start(f32[5,20,4,4,1,1]{1,3,5,4,2,0:T(4,128)} %copy.790), channel_id=1, source_target_pairs={{16,0},{32,16},{48,32},{64,48},{80,64},{96,80},{112,96},{128,112},... | collective-permute-start | bytes 19208 | tf_op jit(solution)/shard_map/ppermute | solution.py:27
  27.7 1.7 copy-start.7
  27.7 1.7 copy-start.24
  31.7 0.9 copy-start.22
  31.7 3.8 %copy-start.25 = (s32[4,1,128]{2,1,0:T(1,128)S(1)}, s32[4,1,128]{2,1,0:T(1,128)}, u32[]{:S(2)}) copy-start(s32[4,1,128]{2,1,0:T(1,128)} %param.14) | copy-start | bytes 6148
  42.8 7.5 %copy-start.2 = (f32[5,20,4,4,1,1]{5,0,3,1,4,2:T(8,128)S(1)}, f32[5,20,4,4,1,1]{5,0,3,1,4,2:T(8,128)}, u32[]{:S(2)}) copy-start(f32[5,20,4,4,1,1]{5,0,3,1,4,2:T(8,128)} %copy.791) | copy-start | bytes 19204
  42.8 7.5 %copy-start.23 = (pred[128]{0:T(512)(128)(4,1)S(1)}, pred[128]{0:T(512)(128)(4,1)}, u32[]{:S(2)}) copy-start(pred[128]{0:T(512)(128)(4,1)} %get-tuple-element.982) | copy-start | bytes 388
  43.5 37.0 %collective-permute-start.2 = (f32[5,20,4,4,1,130]{5,3,4,2,1,0:T(4,128)S(1)}, f32[5,20,4,4,1,130]{5,3,4,2,1,0:T(4,128)S(1)}, u32[]{:S(2)}, u32[]{:S(2)}) collective-permute-start(f32[5,20,4,4,1,130]{5,3,4,2,1,0:T(4,128)S(1)} %copy.793), channel_id=1, source_target_pairs={{0,4},{4,8},{8,12},{12,0},{1,5},{5,9},{9,13},{13,1},{2,6},{6,10},{... | collective-permute-start | bytes 2496008 | tf_op jit(solution)/shard_map/ppermute | solution.py:26
  46.7 36.9 %collective-permute-start.3 = (f32[5,20,4,4,1,130]{5,3,4,2,1,0:T(4,128)S(1)}, f32[5,20,4,4,1,130]{5,3,4,2,1,0:T(4,128)S(1)}, u32[]{:S(2)}, u32[]{:S(2)}) collective-permute-start(f32[5,20,4,4,1,130]{5,3,4,2,1,0:T(4,128)S(1)} %copy.793), channel_id=1, source_target_pairs={{4,0},{8,4},{12,8},{0,12},{5,1},{9,5},{13,9},{1,13},{6,2},{10,6},{... | collective-permute-start | bytes 2496008 | tf_op jit(solution)/shard_map/ppermute | solution.py:27
  50.3 0.6 copy-start.29
  51.0 0.8 copy-start.28
  52.5 28.8 %copy-start.27 = (pred[128]{0:T(512)(128)(4,1)S(1)}, pred[128]{0:T(512)(128)(4,1)}, u32[]{:S(2)}) copy-start(pred[128]{0:T(512)(128)(4,1)} %get-tuple-element.963) | copy-start | bytes 388
  81.4 3.1 %copy-start.26 = (pred[128]{0:T(512)(128)(4,1)S(1)}, pred[128]{0:T(512)(128)(4,1)}, u32[]{:S(2)}) copy-start(pred[128]{0:T(512)(128)(4,1)} %get-tuple-element.964) | copy-start | bytes 388
  84.5 1.0 copy-start.15
  84.5 1.1 copy-start.16
  84.5 1.2 copy-start.17
  84.5 1.2 copy-start.18
  86.6 1.3 copy-start.8
  86.6 1.5 copy-start.19
  86.6 1.5 copy-start.30
  86.6 1.5 copy-start.31
  90.4 16.2 %copy-start.9 = (f32[4,80,1,4,1,128]{5,4,3,2,1,0:T(1,128)S(1)}, f32[4,80,1,4,1,128]{5,4,3,2,1,0:T(1,128)}, u32[]{:S(2)}) copy-start(f32[4,80,1,4,1,128]{5,4,3,2,1,0:T(1,128)} %param.15) | copy-start | bytes 1966084
  90.4 16.1 %copy-start.21 = (f32[1,4,1,128]{3,2,1,0:T(1,128)S(1)}, f32[1,4,1,128]{3,2,1,0:T(1,128)}, u32[]{:S(2)}) copy-start(f32[1,4,1,128]{3,2,1,0:T(1,128)} %param.16) | copy-start | bytes 6148
  91.3 29.7 %all-to-all-start = ((f32[4,2,20,1,4,1,128]{6,4,2,1,5,3,0:T(4,128)}), f32[4,2,20,1,4,1,128]{6,4,2,1,5,3,0:T(4,128)S(1)}, u32[]{:S(2)}, u32[]{:S(2)}) async-start(f32[4,2,20,1,4,1,128]{6,4,2,1,5,3,0:T(4,128)} %pad_maximum_fusion.11), calls=%async_computation | async-start | bytes 655360 | tf_op jit(solution)/shard_map/all_to_all | solution.py:15
  106.7 22.9 %copy-start.14 = (f32[80,1,4,1,128]{4,2,3,1,0:T(4,128)}, f32[80,1,4,1,128]{4,2,3,1,0:T(4,128)S(1)}, u32[]{:S(2)}) copy-start(f32[80,1,4,1,128]{4,2,3,1,0:T(4,128)S(1)} %bitcast_add_fusion) | copy-start | bytes 491524
  106.8 15.7 %copy-start.3 = (f32[1,80,1,4,1,128]{5,3,4,2,1,0:T(4,128)}, f32[1,80,1,4,1,128]{5,3,4,2,1,0:T(4,128)S(1)}, u32[]{:S(2)}) copy-start(f32[1,80,1,4,1,128]{5,3,4,2,1,0:T(4,128)S(1)} %get-tuple-element.716) | copy-start | bytes 491524
  106.9 22.7 %copy-start.5 = (f32[1,80,1,4,1,128]{5,3,4,2,1,0:T(4,128)}, f32[1,80,1,4,1,128]{5,3,4,2,1,0:T(4,128)S(1)}, u32[]{:S(2)}) copy-start(f32[1,80,1,4,1,128]{5,3,4,2,1,0:T(4,128)S(1)} %get-tuple-element.719) | copy-start | bytes 491524
  106.9 22.7 %copy-start.10 = (f32[1,80,1,4,1,128]{5,3,4,2,1,0:T(4,128)}, f32[1,80,1,4,1,128]{5,3,4,2,1,0:T(4,128)S(1)}, u32[]{:S(2)}) copy-start(f32[1,80,1,4,1,128]{5,3,4,2,1,0:T(4,128)S(1)} %get-tuple-element.718) | copy-start | bytes 491524
  106.9 22.7 %copy-start.13 = (f32[1,80,1,4,1,128]{5,3,4,2,1,0:T(4,128)}, f32[1,80,1,4,1,128]{5,3,4,2,1,0:T(4,128)S(1)}, u32[]{:S(2)}) copy-start(f32[1,80,1,4,1,128]{5,3,4,2,1,0:T(4,128)S(1)} %get-tuple-element.717) | copy-start | bytes 491524
  121.2 8.3 %copy-start.11 = (f32[80,1,4,1,128]{4,2,3,1,0:T(4,128)}, f32[80,1,4,1,128]{4,2,3,1,0:T(4,128)S(1)}, u32[]{:S(2)}) copy-start(f32[80,1,4,1,128]{4,2,3,1,0:T(4,128)S(1)} %multiply_subtract_fusion) | copy-start | bytes 491524
  122.6 21.8 %copy-start.4 = (f32[1,80,1,4,1,128]{5,3,4,2,1,0:T(4,128)S(1)}, f32[1,80,1,4,1,128]{5,3,4,2,1,0:T(4,128)}, u32[]{:S(2)}) copy-start(f32[1,80,1,4,1,128]{5,3,4,2,1,0:T(4,128)} %copy-done.3) | copy-start | bytes 491524
  130.2 15.1 %copy-start.6 = (f32[1,80,1,4,1,128]{5,3,4,2,1,0:T(4,128)S(1)}, f32[1,80,1,4,1,128]{5,3,4,2,1,0:T(4,128)}, u32[]{:S(2)}) copy-start(f32[1,80,1,4,1,128]{5,3,4,2,1,0:T(4,128)} %copy-done.5) | copy-start | bytes 491524
  130.3 17.2 %copy-start.12 = (f32[80,1,4,1,128]{4,2,3,1,0:T(4,128)S(1)}, f32[80,1,4,1,128]{4,2,3,1,0:T(4,128)}, u32[]{:S(2)}) copy-start(f32[80,1,4,1,128]{4,2,3,1,0:T(4,128)} %copy-done.11) | copy-start | bytes 491524
  151.8 24.8 %all-to-all-start.1 = ((f32[2,80,1,4,1,128]{5,3,4,2,0,1:T(4,128)}), f32[2,80,1,4,1,128]{5,3,4,2,0,1:T(4,128)S(1)}, u32[]{:S(2)}, u32[]{:S(2)}) async-start(f32[2,80,1,4,1,128]{5,3,4,2,0,1:T(4,128)} %pad_maximum_fusion.12), calls=%async_computation.1 | async-start | bytes 655360 | tf_op jit(solution)/shard_map/all_to_all | solution.py:170
